TPU v7x, 256 devices: a whole 4x4x8 slice. The times are simulated.
256 devices in a mesh: tm: 8 (over z), seq: 32 (over y, x, core).
Axes of the slice: x: 4, y: 4, z: 8, core: 2. Of those that a mesh axis runs over, the one named last changes fastest.
Arguments:
- states: float32 [64, 1536, 64], P('tm', 'seq'), may hold values from -11 to 11
- first_state: float32 [1536, 64], P('seq'), may hold values from -6 to 6
- now_step: int32 [64], P('tm'), may hold values from 1 to 960, as said below
- next_step: int32 [64], P('tm'), may hold values from 0 to 959, as said below
- embed_weight: bfloat16 [64, 1536], replicated, may hold values from -0.75 to 0.75
- mod_weight: bfloat16 [256, 4608], replicated, may hold values from -0.375 to 0.375
- qkv_weight: bfloat16 [1536, 12, 384], P('seq'), may hold values from -1 to 1
- out_weight: bfloat16 [1536, 1536], P('seq'), may hold values from -0.15625 to 0.15625
- final_weight: bfloat16 [1536, 64], replicated, may hold values from -0.15625 to 0.15625
Outputs:
- advanced: float32 [64, 1536, 64], P('tm', 'seq')
- errors: float32 [64], P('tm')
Inputs may be any that keep to these rules, and one draw needn't show every extreme that they name: now_step[0] = 960 and now_step[j + 1] = next_step[j]. next_step[j] is now_step[j] minus a gap of 1 to 15.
All inputs are finite; a program needn't handle non-finite values.
Results may differ from a plain program's by a relative error of at most 0.002.
Values may be sent and summed in bfloat16 or wider, within the bound.
A program may use at most 64 MiB of HBM per device.

v0:
```python
import math

import jax
import jax.numpy as jnp
from jax import lax
from jax.sharding import PartitionSpec as P


def from_behind(shard, axis, by):
    count = lax.axis_size(axis)
    pairs = [(i, i + by) for i in range(count) if 0 <= i + by < count]
    return lax.ppermute(shard, axis, pairs)


def entering(part, axis, combine, identity):
    place = lax.axis_index(axis)
    gathered = lax.all_gather(part, axis)
    state = jnp.zeros_like(part) + jnp.asarray(identity, part.dtype)

    def one(step, state):
        return combine(state, lax.dynamic_index_in_dim(gathered, step, 0, False))

    return lax.fori_loop(0, place, one, state)


def layer_norm(rows):
    row_mean = jnp.mean(rows, axis=-1, keepdims=True)
    centered = rows - row_mean
    variance = jnp.mean(centered * centered, axis=-1, keepdims=True)
    return centered * lax.rsqrt(variance + 1e-06)


def alpha_bar(step_ids):
    fraction = (step_ids.astype(jnp.float32) / 1000.0 + 0.008) / 1.008
    return jnp.cos(fraction * (math.pi / 2)) ** 2


def coefficients(now_step, next_step):
    alpha_now = alpha_bar(now_step)
    alpha_next = alpha_bar(next_step)
    step_ratio = jnp.sqrt(alpha_next / alpha_now)
    keep_coef = step_ratio - 1.0
    noise_coef = jnp.sqrt(1.0 - alpha_next) - step_ratio * jnp.sqrt(1.0 - alpha_now)
    return (keep_coef, noise_coef)


def modulation(step_ids, mod_weight):
    half_freq = mod_weight.shape[0] // 2
    frequency = jnp.exp(-math.log(10000.0) * jnp.arange(half_freq, dtype=jnp.float32) / half_freq)
    angles = step_ids.astype(jnp.float32)[:, None] * frequency[None, :]
    time_embed = jnp.concatenate([jnp.cos(angles), jnp.sin(angles)], axis=1).astype(jnp.bfloat16)
    return jnp.dot(time_embed, mod_weight, preferred_element_type=jnp.float32)


def attend_one(pair_item):
    hdim = pair_item.shape[1] // 3
    length = pair_item.shape[0]
    query_rows = 512
    queries = pair_item[:, :hdim]
    key_rows = pair_item[:, hdim : 2 * hdim]
    values = pair_item[:, 2 * hdim :]

    def one_block(query_block):
        scores = jnp.dot(query_block, key_rows.T, preferred_element_type=jnp.float32) * hdim ** (
            -0.5
        )
        row_max = jnp.max(scores, axis=1, keepdims=True)
        exponent = jnp.exp(scores - row_max)
        weights = (exponent / jnp.sum(exponent, axis=1, keepdims=True)).astype(jnp.bfloat16)
        return jnp.dot(weights, values, preferred_element_type=jnp.float32).astype(jnp.bfloat16)

    blocks_out = lax.map(one_block, queries.reshape(length // query_rows, query_rows, hdim))
    return blocks_out.reshape(length, hdim)


def attend_pairs(pair_block):
    return lax.map(attend_one, pair_block[0])[None]


def add_terms(earlier, later):
    return earlier + later


def per_device(
    states,
    first_state,
    now_step,
    next_step,
    embed_weight,
    mod_weight,
    qkv_weight,
    out_weight,
    final_weight,
):
    step_count, tokd, chans = states.shape
    seq_devs = lax.axis_size("seq")
    time_index = lax.axis_index("tm")
    heads = qkv_weight.shape[1]
    width_three = qkv_weight.shape[2]
    hdim = width_three // 3
    width = heads * hdim
    edge_state = from_behind(states[-1], "tm", 1)
    opening = jnp.where(time_index == 0, first_state, edge_state)
    previous = jnp.concatenate([opening[None], states[:-1]], axis=0)
    keep_coef, noise_coef = coefficients(now_step, next_step)
    modulated_all = modulation(now_step, mod_weight)
    shift_mod = modulated_all[:, :width]
    scale_mod = modulated_all[:, width : 2 * width]
    gate_mod = modulated_all[:, 2 * width :]
    residual = jnp.einsum(
        "tsc,cd->tsd",
        previous.astype(jnp.bfloat16),
        embed_weight,
        preferred_element_type=jnp.float32,
    )
    modulated = (
        layer_norm(residual) * (1.0 + scale_mod[:, None, :]) + shift_mod[:, None, :]
    ).astype(jnp.bfloat16)
    columns = modulated
    projected = jnp.einsum(
        "tsd,dhc->thsc",
        columns,
        lax.all_gather(qkv_weight, "seq", axis=0, tiled=True),
        preferred_element_type=jnp.float32,
    ).astype(jnp.bfloat16)
    pair_count = step_count * heads
    per_dev = pair_count // seq_devs
    grouped = projected.reshape(seq_devs, per_dev, tokd, width_three)
    routed = attend_pairs(lax.all_to_all(grouped, "seq", split_axis=0, concat_axis=2, tiled=True))
    returned = lax.all_to_all(routed, "seq", split_axis=2, concat_axis=0, tiled=True)
    flattened = jnp.transpose(
        returned.reshape(step_count, heads, tokd, hdim), (0, 2, 1, 3)
    ).reshape(step_count, tokd, width)
    columns = flattened
    projection = jnp.einsum(
        "tsd,de->tse",
        columns,
        lax.all_gather(out_weight, "seq", axis=0, tiled=True),
        preferred_element_type=jnp.float32,
    )
    updated = residual + gate_mod[:, None, :] * projection
    normed_out = layer_norm(updated).astype(jnp.bfloat16)
    noise_pred = jnp.einsum(
        "tsd,dc->tsc", normed_out, final_weight, preferred_element_type=jnp.float32
    )
    drift_terms = keep_coef[:, None, None] * previous + noise_coef[:, None, None] * noise_pred
    running_sums = jnp.cumsum(drift_terms, axis=0)
    block_total = running_sums[-1]
    carried = entering(block_total, "tm", add_terms, jnp.zeros_like(block_total))
    advanced = first_state[None] + carried[None] + running_sums
    difference = advanced - states
    partial_value = jnp.sum(difference * difference, axis=(1, 2))
    errors = lax.psum(partial_value, "seq") / (tokd * seq_devs * chans)
    return (advanced, errors)


def solution(mesh):
    in_specs = (
        P("tm", "seq", None),
        P("seq", None),
        P("tm"),
        P("tm"),
        P(),
        P(),
        P("seq", None, None),
        P("seq", None),
        P(),
    )
    out_specs = (P("tm", "seq", None), P("tm"))
    return jax.shard_map(
        per_device, mesh=mesh, in_specs=in_specs, out_specs=out_specs, check_vma=False
    )
```

profile of v0, /device:TPU:1, one launch (start us, length us, event | category | flops | bytes accessed | tf_op | source)
XLA Modules:
  0.0 330.8 jit_solution(13507943861712329472)
XLA Ops:
  8.8 4.3 %collective-permute-start = (f32[48,64]{1,0:T(8,128)S(1)}, f32[48,64]{1,0:T(8,128)S(1)}, u32[]{:S(2)}, u32[]{:S(2)}) collective-permute-start(f32[48,64]{1,0:T(8,128)S(1)} %slice_bitcast_fusion), channel_id=1, source_target_pairs={{0,32},{32,64},{64,96},{96,128},{128,160},{160,192},{192,224},{1,3... | collective-permute-start | bytes 36872 | tf_op jit(solution)/shard_map/ppermute | solution.py:12
  16.2 1.4 copy-done.1
  18.0 68.3 %all-gather.3.cloned.1.call-done = bf16[1536,12,384]{2,0,1:T(8,128)(2,1)} async-done(((bf16[48,12,384]{2,0,1:T(8,128)(2,1)}), bf16[1536,12,384]{2,0,1:T(8,128)(2,1)}) %all-gather.3.cloned.1.call-update) | async-done | bytes 14155792 | tf_op jit(solution)/shard_map/all_gather | solution.py:123
  86.3 11.1 %fusion.18 = bf16[8,48,12,384]{3,1,2,0:T(8,128)(2,1)} fusion(bf16[1536,12,384]{2,0,1:T(8,128)(2,1)} %all-gather.3.cloned.1.call-done, f32[8,48,1536]{2,1,0:T(8,128)} %copy-done.1, f32[8,1536]{1,0:T(8,128)S(1)} %get-tuple-element.105, f32[8,1536]{1,0:T(8,128)S(1)} %get-tuple-element.106, f32[8,48]{1,0:T(8,128)S(1)} %add_rsqrt_fusion.1, ...), kind=kOutput, calls=%fused_computation.20 | convolution fusion | flops 5440536576 | bytes 20155392 | tf_op jit(solution)/shard_map/tsd,dhc->thsc/dot_general | solution.py:120
  97.3 5.5 %all-to-all-start = ((bf16[32,3,48,384]{3,2,1,0:T(8,128)(2,1)}), bf16[32,3,48,384]{3,2,1,0:T(8,128)(2,1)}, u32[]{:S(2)}, u32[]{:S(2)}) async-start(bf16[32,3,48,384]{3,2,1,0:T(8,128)(2,1)} %bitcast.93), calls=%async_computation | async-start | bytes 7077888 | tf_op jit(solution)/shard_map/all_to_all | solution.py:129
  103.6 44.9 %all-to-all-done = bf16[32,3,48,384]{3,2,1,0:T(8,128)(2,1)} async-done(((bf16[32,3,48,384]{3,2,1,0:T(8,128)(2,1)}), bf16[32,3,48,384]{3,2,1,0:T(8,128)(2,1)}, u32[]{:S(2)}, u32[]{:S(2)}) %all-to-all-start) | async-done | bytes 3538976 | tf_op jit(solution)/shard_map/all_to_all | solution.py:129
  148.5 4.1 %copy.17 = bf16[1,3,32,48,384]{4,3,2,1,0:T(8,128)(2,1)} copy(bf16[1,3,32,48,384]{4,3,1,2,0:T(8,128)(2,1)} %bitcast.15) | data formatting | bytes 7077888 | tf_op jit(solution)/shard_map/all_to_all | solution.py:129
  152.6 33.7 %while.31 = (s32[]{:T(128)}, bf16[3,1536,128]{2,1,0:T(8,128)(2,1)}, bf16[3,1536,384]{2,1,0:T(8,128)(2,1)}, s32[]{:T(128)}, s32[]{:T(128)}, /*index=5*/s32[]{:T(128)}) while((s32[]{:T(128)}, bf16[3,1536,128]{2,1,0:T(8,128)(2,1)}, bf16[3,1536,384]{2,1,0:T(8,128)(2,1)}, s32[]{:T(128)}, s32[]{:T(128)}, /*index=5*/s32[]{:T(128)}) %tuple.79), condition=%wide.region_7.8_spmd, body=%wide.region_2.7_spmd.sunk | while | flops 408222720 | bytes 16002250 | solution.py:77
  152.6 1.4 dynamic-slice_bitcast_fusion.2
  154.2 7.8 %while.33 = (s32[]{:T(128)}, bf16[3,512,128]{2,1,0:T(8,128)(2,1)}, bf16[3,512,128]{2,1,0:T(8,128)(2,1)S(1)}, bf16[1536,128]{1,0:T(8,128)(2,1)S(1)}, bf16[1536,128]{1,0:T(8,128)(2,1)S(1)}, /*index=5*/s32[]{:T(128)}) while((s32[]{:T(128)}, bf16[3,512,128]{2,1,0:T(8,128)(2,1)}, bf16[3,512,128]{2,1,0:T(8,128)(2,1)S(1)}, ...), condition=%wide.region_6.6_spmd, body=%wide.region_3.5_spmd.sunk | while | flops 408222720 | bytes 10496585 | solution.py:72
  158.1 1.4 fusion.70
  160.7 1.4 fusion.70
  162.1 1.8 bitcast_dynamic-update-slice_fusion.2
  163.8 1.4 dynamic-slice_bitcast_fusion.2
  165.5 7.8 %while.33 = (s32[]{:T(128)}, bf16[3,512,128]{2,1,0:T(8,128)(2,1)}, bf16[3,512,128]{2,1,0:T(8,128)(2,1)S(1)}, bf16[1536,128]{1,0:T(8,128)(2,1)S(1)}, bf16[1536,128]{1,0:T(8,128)(2,1)S(1)}, /*index=5*/s32[]{:T(128)}) while((s32[]{:T(128)}, bf16[3,512,128]{2,1,0:T(8,128)(2,1)}, bf16[3,512,128]{2,1,0:T(8,128)(2,1)S(1)}, ...), condition=%wide.region_6.6_spmd, body=%wide.region_3.5_spmd.sunk | while | flops 408222720 | bytes 10496585 | solution.py:72
  166.7 1.4 fusion.70
  169.3 1.4 fusion.70
  171.9 1.4 fusion.70
  173.3 1.8 bitcast_dynamic-update-slice_fusion.2
  175.1 1.4 dynamic-slice_bitcast_fusion.2
  176.7 7.8 %while.33 = (s32[]{:T(128)}, bf16[3,512,128]{2,1,0:T(8,128)(2,1)}, bf16[3,512,128]{2,1,0:T(8,128)(2,1)S(1)}, bf16[1536,128]{1,0:T(8,128)(2,1)S(1)}, bf16[1536,128]{1,0:T(8,128)(2,1)S(1)}, /*index=5*/s32[]{:T(128)}) while((s32[]{:T(128)}, bf16[3,512,128]{2,1,0:T(8,128)(2,1)}, bf16[3,512,128]{2,1,0:T(8,128)(2,1)S(1)}, ...), condition=%wide.region_6.6_spmd, body=%wide.region_3.5_spmd.sunk | while | flops 408222720 | bytes 10496585 | solution.py:72
  177.9 1.4 fusion.70
  180.6 1.4 fusion.70
  183.2 1.4 fusion.70
  184.6 1.8 bitcast_dynamic-update-slice_fusion.2
  186.3 8.1 %copy.31 = bf16[3,1536,128]{2,0,1:T(4,128)(2,1)} copy(bf16[3,1536,128]{2,1,0:T(8,128)(2,1)} %get-tuple-element.69) | data formatting | bytes 2359296 | tf_op jit(solution)/shard_map/while | solution.py:77
  194.4 7.4 %all-to-all-start.1 = ((bf16[1,3,1536,128]{3,1,0,2:T(4,128)(2,1)}), bf16[1,3,1536,128]{3,1,0,2:T(4,128)(2,1)}, u32[]{:S(2)}, u32[]{:S(2)}) async-start(bf16[1,3,1536,128]{3,1,0,2:T(4,128)(2,1)} %bitcast.91), calls=%async_computation.1 | async-start | bytes 3145728 | tf_op jit(solution)/shard_map/all_to_all | solution.py:130
  202.0 22.2 %all-to-all-done.1 = bf16[1,3,1536,128]{3,1,0,2:T(4,128)(2,1)} async-done(((bf16[1,3,1536,128]{3,1,0,2:T(4,128)(2,1)}), bf16[1,3,1536,128]{3,1,0,2:T(4,128)(2,1)}, u32[]{:S(2)}, u32[]{:S(2)}) %all-to-all-start.1) | async-done | bytes 1179680 | tf_op jit(solution)/shard_map/all_to_all | solution.py:130
  224.2 1.6 copy.19
  225.9 5.1 %fusion.55 = (f32[8,48]{1,0:T(8,128)S(1)}, f32[8,48,1536]{2,1,0:T(8,128)S(1)}) fusion(f32[8,48,1536]{2,1,0:T(8,128)} %copy-done.1, bf16[1536,1536]{1,0:T(8,128)(2,1)} %all-gather.5.cloned.1.call-done, bf16[8,12,6,8,128]{4,3,2,1,0:T(8,128)(2,1)S(1)} %bitcast.94, f32[8,1536]{1,0:T(8,128)} %get-tuple-element.104), kind=kOutput, calls=%fused_computation.77 | convolution fusion | flops 1813708416 | bytes 10667520 | tf_op jit(solution)/shard_map/tsd,de->tse/dot_general | solution.py:135
  232.6 20.1 %all_gather.11 = f32[8,48,64]{2,1,0:T(8,128)S(1)} all-gather(f32[1,48,64]{2,1,0:T(8,128)S(1)} %slice.39), channel_id=1, replica_groups=mesh['tm'=8,'seq'=32] {'tm'}, dimensions={0}, use_global_device_ids=true | all-gather | bytes 110592 | tf_op jit(solution)/shard_map/all_gather | solution.py:17
  253.5 70.0 %psum.7 = f32[8]{0:T(128)S(1)} all-reduce(f32[8]{0:T(128)S(1)} %get-tuple-element.95), channel_id=1, replica_groups=mesh['tm'=8,'seq'=32] {'seq'}, use_global_device_ids=true, to_apply=%region_14.15 | all-reduce | flops 8 | bytes 64 | tf_op jit(solution)/shard_map/psum | solution.py:153
  (85 shorter events, 21.7 us)
Async XLA Ops:
  7.2 6.7 %copy-start = (bf16[256,4608]{1,0:T(8,128)(2,1)S(1)}, bf16[256,4608]{1,0:T(8,128)(2,1)}, u32[]{:S(2)}) copy-start(bf16[256,4608]{1,0:T(8,128)(2,1)} %param.20) | copy-start | bytes 7077892
  7.2 7.8 %copy-start.4 = (f32[8,48,64]{2,1,0:T(8,128)S(1)}, f32[8,48,64]{2,1,0:T(8,128)}, u32[]{:S(2)}) copy-start(f32[8,48,64]{2,1,0:T(8,128)} %param.15) | copy-start | bytes 294916
  7.2 7.8 %copy-start.10 = (f32[48,64]{1,0:T(8,128)S(1)}, f32[48,64]{1,0:T(8,128)}, u32[]{:S(2)}) copy-start(f32[48,64]{1,0:T(8,128)} %param.16) | copy-start | bytes 36868
  7.2 8.4 %copy-start.9 = (bf16[64,1536]{1,0:T(8,128)(2,1)S(1)}, bf16[64,1536]{1,0:T(8,128)(2,1)}, u32[]{:S(2)}) copy-start(bf16[64,1536]{1,0:T(8,128)(2,1)} %param.19) | copy-start | bytes 589828
  7.2 79.0 %all-gather.3.cloned.1.call-start = ((), (), s32[]{:S(2)}) async-start(), calls=%async_computation.2 | async-start | bytes 14598144 | tf_op jit(solution)/shard_map/all_gather | solution.py:123
  8.8 6.2 %collective-permute-start = (f32[48,64]{1,0:T(8,128)S(1)}, f32[48,64]{1,0:T(8,128)S(1)}, u32[]{:S(2)}, u32[]{:S(2)}) collective-permute-start(f32[48,64]{1,0:T(8,128)S(1)} %slice_bitcast_fusion), channel_id=1, source_target_pairs={{0,32},{32,64},{64,96},{96,128},{128,160},{160,192},{192,224},{1,3... | collective-permute-start | bytes 36872 | tf_op jit(solution)/shard_map/ppermute | solution.py:12
  15.0 3.0 copy-start.2
  15.0 0.6 copy-start.6
  16.2 1.4 copy-start.1
  97.3 51.2 %all-to-all-start = ((bf16[32,3,48,384]{3,2,1,0:T(8,128)(2,1)}), bf16[32,3,48,384]{3,2,1,0:T(8,128)(2,1)}, u32[]{:S(2)}, u32[]{:S(2)}) async-start(bf16[32,3,48,384]{3,2,1,0:T(8,128)(2,1)} %bitcast.93), calls=%async_computation | async-start | bytes 7077888 | tf_op jit(solution)/shard_map/all_to_all | solution.py:129
  102.8 123.1 %all-gather.5.cloned.1.call-start = ((), (), s32[]{:S(2)}) async-start(), calls=%async_computation.3 | async-start | bytes 4866048 | tf_op jit(solution)/shard_map/all_gather | solution.py:138
  186.3 15.5 %copy-start.12 = (s32[8]{0:T(128)S(1)}, s32[8]{0:T(128)}, u32[]{:S(2)}) copy-start(s32[8]{0:T(128)} %param.17) | copy-start | bytes 100
  186.3 15.5 %copy-start.13 = (s32[8]{0:T(128)S(1)}, s32[8]{0:T(128)}, u32[]{:S(2)}) copy-start(s32[8]{0:T(128)} %param.18) | copy-start | bytes 100
  194.4 29.8 %all-to-all-start.1 = ((bf16[1,3,1536,128]{3,1,0,2:T(4,128)(2,1)}), bf16[1,3,1536,128]{3,1,0,2:T(4,128)(2,1)}, u32[]{:S(2)}, u32[]{:S(2)}) async-start(bf16[1,3,1536,128]{3,1,0,2:T(4,128)(2,1)} %bitcast.91), calls=%async_computation.1 | async-start | bytes 3145728 | tf_op jit(solution)/shard_map/all_to_all | solution.py:130
  231.0 0.9 copy-start.8
  231.1 1.5 copy-start.3
  231.1 1.4 copy-start.7
  231.5 21.3 %copy-start.11 = (f32[48,64]{1,0:T(8,128)S(1)}, f32[48,64]{1,0:T(8,128)}, u32[]{:S(2)}) copy-start(f32[48,64]{1,0:T(8,128)} %param.16) | copy-start | bytes 36868
  231.5 21.3 %copy-start.5 = (f32[8,48,64]{2,1,0:T(8,128)S(1)}, f32[8,48,64]{2,1,0:T(8,128)}, u32[]{:S(2)}) copy-start(f32[8,48,64]{2,1,0:T(8,128)} %param.15) | copy-start | bytes 294916
Sparse Core Ops, SparseCore 0:
  10.7 75.5 all-gather.2
  106.2 68.7 all-gather.4
where the time goes:
time: 331 us
  waiting for transfers between devices  137 us (41%)
  blocking collectives  90.1 us (27%)
  matrix products  36 us (11%)
  local copies, waits for them, and re-layouts  27.4 us (8%)
  starting transfers between devices  17.3 us (5%)
  between operations  14.4 us (4%)
  other arithmetic  8.79 us (3%)
    psum x1, blocking collectives, per_device(): errors = lax.psum(partial_value, 'seq') / (tokd * seq_devs * chans)  70 us
    all_gather x1, waiting for transfers between devices, per_device(): lax.all_gather(qkv_weight, 'seq', axis=0, tiled=True)  68.3 us
    all_to_all x1, waiting for transfers between devices, per_device(): lax.all_to_all(grouped, 'seq', split_axis=0, concat_axis=2, tiled=True)  44.9 us
    all_to_all x1, waiting for transfers between devices, per_device(): lax.all_to_all(routed, 'seq', split_axis=2, concat_axis=0, tiled=True)  22.2 us
    all_gather x1, blocking collectives, entering(): gathered = lax.all_gather(part, axis)  20.1 us
    dot_general x9, matrix products, one_block(): jnp.dot(weights, values, preferred_element_type=jnp.float32)  12.4 us
    dot_general x1, matrix products, per_device(): jnp.einsum('tsd,dhc->thsc', columns, lax.all_gather(qkv_weight, 'seq', ax...  11.1 us
    while x1, local copies, waits for them, and re-layouts, attend_pairs(): return lax.map(attend_one, pair_block[0])[None]  8.06 us
  transfers between devices with their start and end apart: 5, of which 3 were waited for; matrix products, arithmetic and copies ran while one was open for 15% of the time, Pallas kernels for 0%

commit v1 on v0

v1 whole, which is shorter than its diff:
```python
import math

import jax
import jax.numpy as jnp
from jax import lax
from jax.experimental import pallas as pl
from jax.experimental.pallas import tpu as pltpu
from jax.sharding import PartitionSpec as P

MESH = pl.DeviceIdType.MESH
F32 = jnp.float32
BF16 = jnp.bfloat16

PLANES = 8
ROWS = 4
COLS = 4
PEERS = 32
STEPS = 8
TOK = 48
PACK = 16
CH = 64
D = 1536
HD = 128
HEADS = 12
GROUP = 3
QTOK = 384
QROW = 128
LANES = 256


def alpha_bar(step_ids):
    fraction = (step_ids.astype(F32) / 1000.0 + 0.008) / 1.008
    return jnp.cos(fraction * (math.pi / 2)) ** 2


def coefficients(now_step, next_step):
    alpha_now = alpha_bar(now_step)
    alpha_next = alpha_bar(next_step)
    step_ratio = jnp.sqrt(alpha_next / alpha_now)
    keep_coef = step_ratio - 1.0
    noise_coef = jnp.sqrt(1.0 - alpha_next) - step_ratio * jnp.sqrt(1.0 - alpha_now)
    return (keep_coef, noise_coef)


def modulation(step_ids, mod_weight):
    half_freq = mod_weight.shape[0] // 2
    frequency = jnp.exp(-math.log(10000.0) * jnp.arange(half_freq, dtype=F32) / half_freq)
    angles = step_ids.astype(F32)[:, None] * frequency[None, :]
    time_embed = jnp.concatenate([jnp.cos(angles), jnp.sin(angles)], axis=1).astype(BF16)
    return jnp.dot(time_embed, mod_weight, preferred_element_type=F32)


def await_bytes(ref, sem):
    pltpu.make_async_copy(ref, ref, sem).wait()


def layer_norm(rows):
    row_mean = jnp.mean(rows, axis=-1, keepdims=True)
    centered = rows - row_mean
    variance = jnp.mean(centered * centered, axis=-1, keepdims=True)
    return centered * lax.rsqrt(variance + 1e-06)


def pack(tokens):
    first = jnp.concatenate([tokens[0:PACK], tokens[PACK : 2 * PACK]], axis=1)
    second = jnp.concatenate([tokens[2 * PACK :], jnp.zeros((PACK, CH), F32)], axis=1)
    return jnp.concatenate([first, second], axis=1)


class Spread:
    def __init__(self, place, pieces, whole, recv, send, send_y, natural):
        self.z, self.x, self.y, self.c, self.parity = place
        self.pieces, self.whole, self.natural = pieces, whole, natural
        self.recv, self.send, self.send_y = recv, send, send_y

    def up(self, k):
        return self.parity + 2 * k if k < 2 else (1 - self.parity) + 2 * (k - 2)

    def slot(self, k, xx, cc):
        major = lax.rem(self.y + self.up(k), ROWS) if self.natural else k
        return major * 8 + xx * 2 + cc

    def rows(self, slot):
        return self.whole.at[pl.ds(pl.multiple_of(slot * TOK, 16), TOK)]

    def await_slot(self, slot):
        await_bytes(self.rows(slot), self.recv.at[slot])

    def stage_y(self):
        for k in range(2):
            up = self.up(k)
            target = lax.rem(self.y - up + ROWS, ROWS)
            here = self.slot(k, self.x, self.c)
            there = (self.y if self.natural else k) * 8 + self.x * 2 + self.c
            source = self.pieces.at[target] if self.pieces.shape[0] > 1 else self.pieces.at[0]

            def remote():
                pltpu.make_async_remote_copy(
                    source, self.rows(there), self.send_y, self.recv.at[there],
                    device_id=(self.z, target * 8 + self.x * 2 + self.c), device_id_type=MESH,
                ).start()

            if k == 0:
                pl.when(self.parity == 1)(remote)

                @pl.when(self.parity == 0)
                def _():
                    pltpu.make_async_copy(source, self.rows(here), self.recv.at[here]).start()
            else:
                remote()

    def pass_on(self, slot, there, plane, xx, cc):
        pltpu.make_async_remote_copy(
            self.rows(slot), self.rows(there), self.send, self.recv.at[there],
            device_id=(plane, self.y * 8 + xx * 2 + cc), device_id_type=MESH,
        ).start()

    def side(self, by):
        return lax.rem(self.x + by + COLS, COLS)

    def to_plane(self, k, xx):
        plane = lax.rem(self.z + (1 if k == 0 else PLANES - 1), PLANES)
        slot = self.slot(k, xx, self.c)
        there = slot if self.natural else slot + 16
        self.pass_on(slot, there, plane, self.x, self.c)

    def to_sibling(self, slot):
        self.pass_on(slot, slot, self.z, self.x, 1 - self.c)

    def own(self, k):
        slot = self.slot(k, self.x, self.c)
        self.await_slot(slot)
        self.pass_on(slot, slot, self.z, self.side(1), self.c)
        self.pass_on(slot, slot, self.z, self.side(-1), self.c)
        self.to_plane(k, self.x)
        self.to_sibling(slot)

    def from_left(self, k):
        slot = self.slot(k, self.side(-1), self.c)
        self.await_slot(slot)
        if k == 0:
            self.pass_on(slot, slot, self.z, self.side(1), self.c)
        self.to_plane(k, self.side(-1))
        self.to_sibling(slot)

    def from_right(self, k):
        slot = self.slot(k, self.side(1), self.c)
        self.await_slot(slot)
        if k == 1:
            self.pass_on(slot, slot, self.z, self.side(-1), self.c)
        self.to_plane(k, self.side(1))
        self.to_sibling(slot)

    def far(self, k):
        slot = self.slot(k, self.side(2), self.c)
        self.await_slot(slot)
        self.to_plane(k, self.side(2))
        self.to_sibling(slot)

    def from_plane(self, k, by):
        slot = self.slot(k, self.side(by), self.c)
        self.await_slot(slot)
        self.to_sibling(slot)

    def await_sibling(self, k):
        for xx in range(COLS):
            self.await_slot(self.slot(k, xx, 1 - self.c))

    def finish(self):
        await_bytes(self.whole.at[pl.ds(0, 30 * TOK)], self.send)
        one = self.whole.at[pl.ds(0, TOK)]
        two = self.whole.at[pl.ds(0, 2 * TOK)]

        @pl.when(self.parity == 0)
        def _():
            await_bytes(one, self.send_y)

        @pl.when(self.parity == 1)
        def _():
            await_bytes(two, self.send_y)


def kernel(
    states, first, mods, coef, embed, qkv_pieces, out_pieces, final, adv_out, err_out,
    packed, messages, latents, edge, embed3, final2, qkv_rows, out_rows, modulated, accum,
    queries, key_rows, values, attended, gathered, updated, noise_own, noise_in, total, totals, part, parts,
    qkv_recv, qkv_send, qkv_send_y, out_recv, out_send, out_send_y,
    latent_recv, latent_send, edge_recv, edge_send, att_recv, att_send,
    noise_recv, noise_send, total_recv, total_send, part_recv, part_send,
):
    z = lax.axis_index("tm")
    s = lax.axis_index("seq")
    c = lax.rem(s, 2)
    x = lax.rem(s // 2, COLS)
    y = s // 8
    j = lax.rem(s, 8)
    parity = lax.rem(z, 2)
    place = (z, x, y, c, parity)
    above = lax.rem(z + 1, PLANES)
    below = lax.rem(z + PLANES - 1, PLANES)

    barrier = pltpu.get_barrier_semaphore()

    def greet(o, carry):
        pl.semaphore_signal(barrier, inc=1, device_id=(z, lax.rem(s + o, PEERS)), device_id_type=MESH)
        return carry

    lax.fori_loop(1, PEERS, greet, 0)

    def greet_column(o, carry):
        pl.semaphore_signal(barrier, inc=1, device_id=(lax.rem(z + o, PLANES), s), device_id_type=MESH)
        return carry

    lax.fori_loop(1, PLANES, greet_column, 0)
    pl.semaphore_signal(barrier, inc=1, device_id=(below, y * 8 + 7), device_id_type=MESH)

    start = pack(first[...])
    for t in range(STEPS):
        block = pack(states[t])
        packed[t] = block
        if t == STEPS - 1:
            block = jnp.where(z == PLANES - 1, start, block)
        messages[t] = block.astype(BF16)
    embed3[...] = jnp.zeros_like(embed3)
    for third in range(3):
        embed3[third, third * CH : (third + 1) * CH, :] = embed[...]
    weight = final[...]
    final2[0] = jnp.concatenate([weight, jnp.zeros((D, CH), BF16)], axis=1)
    final2[1] = jnp.concatenate([jnp.zeros((D, CH), BF16), weight], axis=1)
    for head in range(GROUP):
        values[head, :, HD:] = jnp.ones((D, HD), BF16)

    pl.semaphore_wait(barrier, jnp.where(j == 7, 46, 38))

    def latent_slot(k):
        return latents.at[pl.ds(pl.multiple_of(k * PACK, PACK), PACK)]

    def send_latent(o, carry):
        peer = lax.rem(s + o, PEERS)
        pltpu.make_async_remote_copy(
            messages.at[lax.rem(peer, 8)], latent_slot(s), latent_send, latent_recv,
            device_id=(z, peer), device_id_type=MESH,
        ).start()
        return carry

    lax.fori_loop(1, PEERS, send_latent, 0)
    pltpu.make_async_copy(messages.at[j], latent_slot(s), latent_recv).start()

    qkv = Spread(place, qkv_pieces, qkv_rows, qkv_recv, qkv_send, qkv_send_y, False)
    out = Spread(place, out_pieces, out_rows, out_recv, out_send, out_send_y, True)
    qkv.stage_y()
    edge_copy = pltpu.make_async_remote_copy(
        packed.at[STEPS - 1], edge, edge_send, edge_recv, device_id=(above, s), device_id_type=MESH
    )
    edge_copy.start()
    qkv.own(0)
    qkv.own(1)
    await_bytes(latents, latent_recv)

    def mod_row(kind, start, size):
        return mods[pl.ds(j, 1), pl.ds(pl.multiple_of(kind * D + start, 128), size)]

    def make_modulated(quarter):
        rows = latents[quarter * QROW : (quarter + 1) * QROW, :]

        def one(third, carry):
            chunks = []
            for k in range(4):
                at = lax.rem(y + qkv.up(k), ROWS) * QTOK
                chunks.append(
                    jnp.dot(
                        rows, embed3[third, :, pl.ds(pl.multiple_of(at, 128), QTOK)],
                        preferred_element_type=F32,
                    )
                )
            row_mean = sum(jnp.sum(v, axis=1, keepdims=True) for v in chunks) / D
            chunks = [v - row_mean for v in chunks]
            variance = sum(jnp.sum(v * v, axis=1, keepdims=True) for v in chunks) / D
            inverse = lax.rsqrt(variance + 1e-06)
            base = pl.multiple_of(quarter * QTOK + third * QROW, QROW)
            for k in range(4):
                at = lax.rem(y + qkv.up(k), ROWS) * QTOK
                modulated[pl.ds(base, QROW), k * QTOK : (k + 1) * QTOK] = (
                    chunks[k] * inverse * (1.0 + mod_row(1, at, QTOK)) + mod_row(0, at, QTOK)
                ).astype(BF16)
            return carry

        lax.fori_loop(0, 3, one, 0)

    make_modulated(0)
    qkv.from_left(0)
    qkv.from_right(0)
    make_modulated(1)
    qkv.from_left(1)
    qkv.from_right(1)
    make_modulated(2)
    qkv.far(0)
    make_modulated(3)
    qkv.far(1)
    out.stage_y()
    qkv.await_sibling(0)
    qkv.await_sibling(1)

    def project_first(i, carry):
        at = pl.ds(pl.multiple_of(i * 256, 256), 256)
        accum[at, :] = jnp.dot(modulated[at, : D // 2], qkv_rows[: D // 2, :], preferred_element_type=F32)
        return carry

    lax.fori_loop(0, 2, project_first, 0)
    for k in (2, 3):
        qkv.from_plane(k, 0)
    lax.fori_loop(2, 4, project_first, 0)
    for k in (2, 3):
        qkv.from_plane(k, -1)
        qkv.from_plane(k, 1)
    lax.fori_loop(4, 6, project_first, 0)
    for k in (2, 3):
        qkv.from_plane(k, 2)
    out.own(0)
    out.own(1)
    qkv.await_sibling(2)
    qkv.await_sibling(3)

    scale = HD ** (-0.5) * math.log2(math.e)

    def project_second(i, carry):
        at = pl.ds(pl.multiple_of(i * 256, 256), 256)
        whole = accum[at, :] + jnp.dot(
            modulated[at, D // 2 :], qkv_rows[D // 2 :, :], preferred_element_type=F32
        )
        for head in range(GROUP):
            base = head * 3 * HD
            queries[head, at, :] = (whole[:, base : base + HD] * scale).astype(BF16)
            key_rows[head, at, :] = whole[:, base + HD : base + 2 * HD].astype(BF16)
            values[head, at, :HD] = whole[:, base + 2 * HD : base + 3 * HD].astype(BF16)
        return carry

    lax.fori_loop(0, 3, project_second, 0)
    out.from_left(0)
    out.from_right(0)
    lax.fori_loop(3, 6, project_second, 0)
    out.from_left(1)
    out.from_right(1)

    def attend(head):
        column = pl.ds(pl.multiple_of((y * GROUP + head) * HD, HD), HD)

        def one(i, carry):
            quarter = lax.rem(y + 1 + i, ROWS)
            block = queries[head, pl.ds(pl.multiple_of(quarter * QTOK, QTOK), QTOK), :]
            scores = lax.dot_general(
                block, key_rows[head], (((1,), (1,)), ((), ())), preferred_element_type=F32
            )
            row_max = jnp.max(scores, axis=1, keepdims=True)
            weights = jnp.exp2(scores - row_max).astype(BF16)
            both = jnp.dot(weights, values[head], preferred_element_type=F32)
            attended[head * ROWS + i] = (both[:, :HD] / both[:, HD:]).astype(BF16)

            @pl.when(i < 3)
            def _():
                pltpu.make_async_remote_copy(
                    attended.at[head * ROWS + i], gathered.at[:, column], att_send, att_recv,
                    device_id=(z, quarter * 8 + j), device_id_type=MESH,
                ).start()

            @pl.when(i == 3)
            def _():
                pltpu.make_async_copy(attended.at[head * ROWS + i], gathered.at[:, column], att_recv).start()

            return carry

        lax.fori_loop(0, ROWS, one, 0)

    attend(0)
    out.far(0)
    out.far(1)
    for k in (2, 3):
        out.from_plane(k, 0)
    attend(1)
    for k in (2, 3):
        out.from_plane(k, -1)
        out.from_plane(k, 1)
        out.from_plane(k, 2)
    attend(2)
    for k in range(4):
        out.await_sibling(k)
    await_bytes(gathered, att_recv)

    for n in range(3):
        at = slice(n * 512, (n + 1) * 512)
        updated[:, at] = jnp.dot(gathered[...], out_rows[:, at], preferred_element_type=F32)

    normed = []
    own_rows = latents[pl.ds(pl.multiple_of(y * QROW, QROW), QROW), :]
    for third in range(3):
        residual = jnp.dot(own_rows, embed3[third], preferred_element_type=F32)
        moved = residual + mod_row(2, 0, D) * updated[third * QROW : (third + 1) * QROW, :]
        normed.append(layer_norm(moved).astype(BF16))
    near = jnp.dot(normed[0], final2[0], preferred_element_type=F32)
    near = near + jnp.dot(normed[1], final2[1], preferred_element_type=F32)
    rest = jnp.dot(normed[2], final2[0], preferred_element_type=F32)
    for k in range(8):
        at = slice(k * PACK, (k + 1) * PACK)
        noise_own[k, :, :HD] = near[at]
        noise_own[k, :, HD:] = rest[at]

    arrive = lax.rem(j + 1, STEPS)
    plane = jnp.where(j == 7, above, z)
    for k in range(8):
        mine = jnp.logical_and(j != 7, j == k)

        @pl.when(jnp.logical_not(mine))
        def _():
            pltpu.make_async_remote_copy(
                noise_own.at[k], noise_in.at[arrive], noise_send, noise_recv,
                device_id=(plane, y * 8 + k), device_id_type=MESH,
            ).start()

        @pl.when(mine)
        def _():
            pltpu.make_async_copy(noise_own.at[k], noise_in.at[arrive], noise_recv).start()

    edge_copy.wait_recv()
    before = jnp.where(z == 0, start, edge[...])
    await_bytes(noise_in, noise_recv)

    running = jnp.zeros((PACK, LANES), F32)
    sums = []
    for t in range(STEPS):
        previous = before if t == 0 else packed[t - 1]
        running = running + (coef[t : t + 1, :] * previous + coef[STEPS + t : STEPS + t + 1, :] * noise_in[t])
        sums.append(running)
    total[...] = running
    for o in range(1, PLANES):

        @pl.when(z + o < PLANES)
        def _():
            pltpu.make_async_remote_copy(
                total, totals.at[z], total_send.at[o], total_recv.at[z],
                device_id=(z + o, s), device_id_type=MESH,
            ).start()

    totals_sum = start
    for o in range(PLANES - 1):

        @pl.when(o < z)
        def _():
            await_bytes(totals.at[o], total_recv.at[o])

        @pl.when(o >= z)
        def _():
            totals[o] = jnp.zeros((PACK, LANES), F32)

        totals_sum = totals_sum + totals[o]

    squares = []
    for t in range(STEPS):
        advanced = totals_sum + sums[t]
        adv_out[t, 0:PACK, :] = advanced[:, 0:CH]
        adv_out[t, PACK : 2 * PACK, :] = advanced[:, CH : 2 * CH]
        adv_out[t, 2 * PACK :, :] = advanced[:, 2 * CH : 3 * CH]
        difference = advanced - packed[t]
        square = jnp.sum(difference * difference, axis=0, keepdims=True)
        squares.append(square[:, :HD] + square[:, HD:])
    part[...] = jnp.concatenate(squares, axis=0)

    def send_part(o, carry):
        pltpu.make_async_remote_copy(
            part, parts.at[s], part_send, part_recv,
            device_id=(z, lax.rem(s + o, PEERS)), device_id_type=MESH,
        ).start()
        return carry

    lax.fori_loop(1, PEERS, send_part, 0)
    pltpu.make_async_copy(part, parts.at[s], part_recv).start()
    await_bytes(parts, part_recv)
    summed = jnp.sum(jnp.sum(parts[...], axis=0), axis=1, keepdims=True) / (D * CH)
    err_out[...] = jnp.broadcast_to(summed, (STEPS, HD))

    qkv.finish()
    out.finish()
    await_bytes(latents.at[pl.ds(0, (PEERS - 1) * PACK)], latent_send)
    edge_copy.wait_send()
    await_bytes(attended.at[pl.ds(0, 9)], att_send)

    @pl.when(j == 7)
    def _():
        await_bytes(noise_in, noise_send)

    @pl.when(j != 7)
    def _():
        await_bytes(noise_in.at[pl.ds(0, 7)], noise_send)

    for o in range(1, PLANES):

        @pl.when(z + o < PLANES)
        def _():
            await_bytes(total, total_send.at[o])

    await_bytes(parts.at[pl.ds(0, PEERS - 1)], part_send)


def per_device(
    states, first_state, now_step, next_step, embed_weight, mod_weight, qkv_weight, out_weight, final_weight
):
    plane = lax.axis_index("tm")
    keep_coef, noise_coef = coefficients(now_step, next_step)
    coef = jnp.broadcast_to(jnp.concatenate([keep_coef, noise_coef])[:, None], (2 * STEPS, LANES))
    last = jnp.logical_and(plane == PLANES - 1, jnp.arange(STEPS) == STEPS - 1)
    mods = modulation(jnp.where(last, 960, next_step), mod_weight)
    qkv_pieces = jnp.transpose(qkv_weight.reshape(TOK, ROWS, GROUP * 3 * HD), (1, 0, 2))
    out_pieces = out_weight[None]
    dma = pltpu.SemaphoreType.DMA
    vmem = pltpu.VMEM
    advanced, errors = pl.pallas_call(
        kernel,
        out_shape=(
            jax.ShapeDtypeStruct((STEPS, TOK, CH), F32),
            jax.ShapeDtypeStruct((STEPS, HD), F32),
        ),
        in_specs=[pl.BlockSpec(memory_space=pltpu.VMEM)] * 8,
        out_specs=(pl.BlockSpec(memory_space=pltpu.VMEM),) * 2,
        scratch_shapes=[
            vmem((STEPS, PACK, LANES), F32),
            vmem((STEPS, PACK, LANES), BF16),
            vmem((PEERS * PACK, LANES), BF16),
            vmem((PACK, LANES), F32),
            vmem((3, LANES, D), BF16),
            vmem((2, D, HD), BF16),
            vmem((D, GROUP * 3 * HD), BF16),
            vmem((D, D), BF16),
            vmem((D, D), BF16),
            vmem((D, GROUP * 3 * HD), F32),
            vmem((GROUP, D, HD), BF16),
            vmem((GROUP, D, HD), BF16),
            vmem((GROUP, D, 2 * HD), BF16),
            vmem((GROUP * ROWS, QTOK, HD), BF16),
            vmem((QTOK, D), BF16),
            vmem((QTOK, D), F32),
            vmem((8, PACK, LANES), F32),
            vmem((STEPS, PACK, LANES), F32),
            vmem((PACK, LANES), F32),
            vmem((PLANES, PACK, LANES), F32),
            vmem((STEPS, HD), F32),
            vmem((PEERS, STEPS, HD), F32),
            dma((PEERS,)), dma, dma,
            dma((PEERS,)), dma, dma,
            dma, dma, dma, dma, dma, dma,
            dma, dma, dma((PLANES,)), dma((PLANES,)), dma, dma,
        ],
        compiler_params=pltpu.CompilerParams(
            collective_id=0, has_side_effects=True, vmem_limit_bytes=60 * 1024 * 1024
        ),
        name="picard",
    )(states, first_state, mods, coef, embed_weight, qkv_pieces, out_pieces, final_weight)
    return advanced, errors[:, 0]


def solution(mesh):
    in_specs = (
        P("tm", "seq", None),
        P("seq", None),
        P("tm"),
        P("tm"),
        P(),
        P(),
        P("seq", None, None),
        P("seq", None),
        P(),
    )
    out_specs = (P("tm", "seq", None), P("tm"))
    return jax.shard_map(
        per_device, mesh=mesh, in_specs=in_specs, out_specs=out_specs, check_vma=False
    )
```

time: 331 us -> 92.4 us (0.28)
  waiting for transfers between devices: 137 us -> 0 us
  blocking collectives: 90.1 us -> 0 us
  Pallas kernels: 0 us -> 80.9 us
  matrix products: 36 us -> 1.08 us
  local copies, waits for them, and re-layouts: 27.4 us -> 7.43 us
  starting transfers between devices: 17.3 us -> 0 us
  between operations: 14.4 us -> 0.7 us
  other arithmetic: 8.79 us -> 1.14 us
    pallas_call x0 -> x1, Pallas kernels: none -> 80.9 us  [per_device(): pl.pallas_call(kernel, out_shape=(jax.ShapeDtypeStruct((STEPS, TOK, CH),...]
    psum x1 -> x0, blocking collectives: 70 us -> none  [per_device(): errors = lax.psum(partial_value, 'seq') / (tokd * seq_devs * chans)]
    all_gather x2 -> x0, waiting for transfers between devices: 68.3 us -> none  [the longest x1 68.3 us: per_device(): lax.all_gather(qkv_weight, 'seq', axis=0, tiled=True)]
    all_to_all x2 -> x0, waiting for transfers between devices: 67.1 us -> none  [the longest x1 44.9 us: per_device(): lax.all_to_all(grouped, 'seq', split_axis=0, concat_axis=2, tiled=True)]
    dot_general x23 -> x1, matrix products: 36 us -> 1.08 us  [modulation(): return jnp.dot(time_embed, mod_weight, preferred_element_type=F32)]
    all_gather x1 -> x0, blocking collectives: 20.1 us -> none  [entering(): gathered = lax.all_gather(part, axis)]
    all_to_all x2 -> x0, starting transfers between devices: 12.9 us -> none  [the longest x1 7.43 us: per_device(): lax.all_to_all(routed, 'seq', split_axis=2, concat_axis=0, tiled=True)]
    while x1 -> x0, local copies, waits for them, and re-layouts: 8.06 us -> none  [attend_pairs(): return lax.map(attend_one, pair_block[0])[None]]
  transfers between devices with their start and end apart: 5 -> 0, of which waited for: 3 -> 0; matrix products, arithmetic and copies ran while one was open for 15% -> 0% of each run, Pallas kernels for 0% -> 0%
where the time goes in v1:
time: 92.4 us; the launch traced here: 91.2 us
  Pallas kernels  80.9 us (88%)
  local copies, waits for them, and re-layouts  7.43 us (8%)
  other arithmetic  1.14 us (1%)
  matrix products  1.08 us (1%)
    pallas_call x1, Pallas kernels, per_device(): pl.pallas_call(kernel, out_shape=(jax.ShapeDtypeStruct((STEPS, TOK, CH),...  80.9 us
    unnamed x11, local copies, waits for them, and re-layouts  4.29 us

profile of v1, /device:TPU:1, one launch (start us, length us, event | category | flops | bytes accessed | tf_op | source)
XLA Modules:
  0.0 91.2 jit_solution(16083912142736869179)
XLA Ops:
  0.6 0.0 copy-start
  0.6 0.0 copy-start.2
  0.7 0.0 copy-start.3
  0.7 0.0 copy-start.1
  0.7 0.8 fusion.6
  1.5 0.1 fusion
  1.6 0.7 copy-done
  2.3 1.1 %fusion.2.mods = f32[8,4608]{1,0:T(8,128)} fusion(bf16[256,4608]{1,0:T(8,128)(2,1)S(1)} %copy-done, bf16[8,128]{1,0:T(8,128)(2,1)S(1)} %get-tuple-element.9, bf16[8,128]{1,0:T(8,128)(2,1)S(1)} %get-tuple-element.8), kind=kOutput, calls=%fused_computation.5 | convolution fusion | flops 18882560 | bytes 2510848 | tf_op jit(solution)/shard_map/dot_general | solution.py:50
  3.4 0.0 copy-done.2
  3.4 0.0 copy-done.3
  3.4 0.1 broadcast_add_fusion
  3.5 0.1 multiply_subtract_fusion
  3.5 0.1 pad_maximum_fusion
  3.6 0.7 broadcast_in_dim.16.coef
  4.3 0.0 copy-done.1
  4.3 0.1 copy.12
  4.4 0.3 reshape.14
  4.7 0.8 copy.16
  5.6 1.9 %copy.14.final = bf16[1536,64]{1,0:T(8,128)(2,1)} copy(bf16[1536,64]{0,1:T(8,128)(2,1)} %param.17) | data formatting | bytes 393216 | tf_op args[8]
  7.4 80.9 %picard.1 = (f32[8,48,64]{2,1,0:T(8,128)}, f32[8,128]{1,0:T(8,128)}) custom-call(f32[8,48,64]{2,1,0:T(8,128)} %states.1, f32[48,64]{1,0:T(8,128)} %first.1, f32[8,4608]{1,0:T(8,128)} %fusion.2.mods, f32[16,256]{1,0:T(8,128)} %broadcast_in_dim.16.coef, bf16[64,1536]{1,0:T(8,128)(2,1)} %embed.1, bf16[4,48,1152]{2,1,0:T(8,128)(2,1)} %bitcast.5, ...), custom_call_target="tpu_custom_call" | custom-call | tf_op jit(solution)/shard_map/picard/pallas_call | solution.py:515
  88.3 1.3 %slice_reduce_fusion = f32[8]{0:T(128)} fusion(f32[8,128]{1,0:T(8,128)} %get-tuple-element.5), kind=kLoop, calls=%fused_computation.9 | loop fusion | bytes 64 | tf_op jit(solution)/shard_map/slice | solution.py:556
  89.6 1.6 %copy.18 = f32[8,48,64]{2,1,0:T(8,128)} copy(f32[8,48,64]{2,1,0:T(8,128)} %get-tuple-element.12) | data formatting | bytes 196608
  (1 shorter events, 0.0 us)
Async XLA Ops:
  0.6 1.7 %copy-start = (bf16[256,4608]{1,0:T(8,128)(2,1)S(1)}, bf16[256,4608]{1,0:T(8,128)(2,1)}, u32[]{:S(2)}) copy-start(bf16[256,4608]{1,0:T(8,128)(2,1)} %param.14) | copy-start | bytes 7077892
  0.6 2.8 %copy-start.2 = (s32[8]{0:T(128)S(1)}, s32[8]{0:T(128)}, u32[]{:S(2)}) copy-start(s32[8]{0:T(128)} %param.12) | copy-start | bytes 100
  0.7 2.7 %copy-start.3 = (s32[8]{0:T(128)S(1)}, s32[8]{0:T(128)}, u32[]{:S(2)}) copy-start(s32[8]{0:T(128)} %param.11) | copy-start | bytes 100
  0.7 3.6 %copy-start.1 = (bf16[48,12,384]{2,0,1:T(8,128)(2,1)S(1)}, bf16[48,12,384]{2,0,1:T(8,128)(2,1)}, u32[]{:S(2)}) copy-start(bf16[48,12,384]{2,0,1:T(8,128)(2,1)} %param.15) | copy-start | bytes 1327108

commit v2 on v1

--- a/solution.py
+++ b/solution.py
@@ -42,12 +42,12 @@
     return (keep_coef, noise_coef)
 
 
-def modulation(step_ids, mod_weight):
-    half_freq = mod_weight.shape[0] // 2
-    frequency = jnp.exp(-math.log(10000.0) * jnp.arange(half_freq, dtype=F32) / half_freq)
-    angles = step_ids.astype(F32)[:, None] * frequency[None, :]
-    time_embed = jnp.concatenate([jnp.cos(angles), jnp.sin(angles)], axis=1).astype(BF16)
-    return jnp.dot(time_embed, mod_weight, preferred_element_type=F32)
+def on_rows(steps):
+    row = lax.broadcasted_iota(jnp.int32, (STEPS, HD), 0)
+    spread = jnp.zeros((STEPS, HD), jnp.int32)
+    for t in range(STEPS):
+        spread = jnp.where(row == t, steps[t], spread)
+    return spread
 
 
 def await_bytes(ref, sem):
@@ -181,12 +181,12 @@
 
 
 def kernel(
-    states, first, mods, coef, embed, qkv_pieces, out_pieces, final, adv_out, err_out,
-    packed, messages, latents, edge, embed3, final2, qkv_rows, out_rows, modulated, accum,
+    states, first, now_step, next_step, embed, mod_weight, qkv_heads, out_pieces, final, adv_out, err_out,
+    mod_rows, mods, coef, qkv_pieces, packed, messages, latents, edge, embed3, final2, qkv_rows, out_rows, modulated, accum,
     queries, key_rows, values, attended, gathered, updated, noise_own, noise_in, total, totals, part, parts,
     qkv_recv, qkv_send, qkv_send_y, out_recv, out_send, out_send_y,
     latent_recv, latent_send, edge_recv, edge_send, att_recv, att_send,
-    noise_recv, noise_send, total_recv, total_send, part_recv, part_send,
+    noise_recv, noise_send, mod_sem, total_recv, total_send, part_recv, part_send,
 ):
     z = lax.axis_index("tm")
     s = lax.axis_index("seq")
@@ -214,6 +214,8 @@
     lax.fori_loop(1, PLANES, greet_column, 0)
     pl.semaphore_signal(barrier, inc=1, device_id=(below, y * 8 + 7), device_id_type=MESH)
 
+    mod_copy = pltpu.make_async_copy(mod_weight, mod_rows, mod_sem)
+    mod_copy.start()
     start = pack(first[...])
     for t in range(STEPS):
         block = pack(states[t])
@@ -224,11 +226,27 @@
     embed3[...] = jnp.zeros_like(embed3)
     for third in range(3):
         embed3[third, third * CH : (third + 1) * CH, :] = embed[...]
-    weight = final[...]
-    final2[0] = jnp.concatenate([weight, jnp.zeros((D, CH), BF16)], axis=1)
-    final2[1] = jnp.concatenate([jnp.zeros((D, CH), BF16), weight], axis=1)
+    final2[...] = jnp.zeros_like(final2)
+    final2[0, :CH, :] = final[...]
+    final2[1, CH:, :] = final[...]
+    for group in range(ROWS):
+        for head in range(GROUP):
+            qkv_pieces[group, :, head * 3 * HD : (head + 1) * 3 * HD] = qkv_heads[group * GROUP + head]
     for head in range(GROUP):
         values[head, :, HD:] = jnp.ones((D, HD), BF16)
+
+    keep_coef, noise_coef = coefficients(on_rows(now_step), on_rows(next_step))
+    for half in range(2):
+        coef[:STEPS, half * HD : (half + 1) * HD] = keep_coef
+        coef[STEPS:, half * HD : (half + 1) * HD] = noise_coef
+    step = jnp.where(jnp.logical_and(z == PLANES - 1, j == STEPS - 1), 960, next_step[j])
+    lane = lax.broadcasted_iota(jnp.int32, (STEPS, HD), 1).astype(F32)
+    angles = step.astype(F32) * jnp.exp(-math.log(10000.0) * lane / HD)
+    time_embed = jnp.concatenate([jnp.cos(angles), jnp.sin(angles)], axis=1).astype(BF16)
+    mod_copy.wait()
+    for n in range(3):
+        at = slice(n * D, (n + 1) * D)
+        mods[:, at] = jnp.dot(time_embed, mod_rows[:, at], preferred_element_type=F32)
 
     pl.semaphore_wait(barrier, jnp.where(j == 7, 46, 38))
 
@@ -255,10 +273,12 @@
     edge_copy.start()
     qkv.own(0)
     qkv.own(1)
+    qkv.from_left(0)
+    qkv.from_right(0)
     await_bytes(latents, latent_recv)
 
     def mod_row(kind, start, size):
-        return mods[pl.ds(j, 1), pl.ds(pl.multiple_of(kind * D + start, 128), size)]
+        return mods[0:1, pl.ds(pl.multiple_of(kind * D + start, 128), size)]
 
     def make_modulated(quarter):
         rows = latents[quarter * QROW : (quarter + 1) * QROW, :]
@@ -288,16 +308,16 @@
         lax.fori_loop(0, 3, one, 0)
 
     make_modulated(0)
-    qkv.from_left(0)
-    qkv.from_right(0)
-    make_modulated(1)
     qkv.from_left(1)
     qkv.from_right(1)
+    make_modulated(1)
+    qkv.far(0)
     make_modulated(2)
-    qkv.far(0)
-    make_modulated(3)
     qkv.far(1)
     out.stage_y()
+    make_modulated(3)
+    qkv.from_plane(2, 0)
+    qkv.from_plane(3, 0)
     qkv.await_sibling(0)
     qkv.await_sibling(1)
 
@@ -307,15 +327,14 @@
         return carry
 
     lax.fori_loop(0, 2, project_first, 0)
-    for k in (2, 3):
-        qkv.from_plane(k, 0)
+    qkv.from_plane(2, -1)
+    qkv.from_plane(2, 1)
     lax.fori_loop(2, 4, project_first, 0)
-    for k in (2, 3):
-        qkv.from_plane(k, -1)
-        qkv.from_plane(k, 1)
+    qkv.from_plane(3, -1)
+    qkv.from_plane(3, 1)
     lax.fori_loop(4, 6, project_first, 0)
-    for k in (2, 3):
-        qkv.from_plane(k, 2)
+    qkv.from_plane(2, 2)
+    qkv.from_plane(3, 2)
     out.own(0)
     out.own(1)
     qkv.await_sibling(2)
@@ -342,11 +361,11 @@
     out.from_left(1)
     out.from_right(1)
 
-    def attend(head):
-        column = pl.ds(pl.multiple_of((y * GROUP + head) * HD, HD), HD)
-
-        def one(i, carry):
-            quarter = lax.rem(y + 1 + i, ROWS)
+    def attend(i):
+        quarter = lax.rem(y + 1 + i, ROWS)
+
+        def one(head, carry):
+            column = pl.ds(pl.multiple_of((y * GROUP + head) * HD, HD), HD)
             block = queries[head, pl.ds(pl.multiple_of(quarter * QTOK, QTOK), QTOK), :]
             scores = lax.dot_general(
                 block, key_rows[head], (((1,), (1,)), ((), ())), preferred_element_type=F32
@@ -354,34 +373,33 @@
             row_max = jnp.max(scores, axis=1, keepdims=True)
             weights = jnp.exp2(scores - row_max).astype(BF16)
             both = jnp.dot(weights, values[head], preferred_element_type=F32)
-            attended[head * ROWS + i] = (both[:, :HD] / both[:, HD:]).astype(BF16)
-
-            @pl.when(i < 3)
-            def _():
+            attended[i * GROUP + head] = (both[:, :HD] / both[:, HD:]).astype(BF16)
+            source = attended.at[i * GROUP + head]
+            if i < 3:
                 pltpu.make_async_remote_copy(
-                    attended.at[head * ROWS + i], gathered.at[:, column], att_send, att_recv,
+                    source, gathered.at[:, column], att_send, att_recv,
                     device_id=(z, quarter * 8 + j), device_id_type=MESH,
                 ).start()
-
-            @pl.when(i == 3)
-            def _():
-                pltpu.make_async_copy(attended.at[head * ROWS + i], gathered.at[:, column], att_recv).start()
-
+            else:
+                pltpu.make_async_copy(source, gathered.at[:, column], att_recv).start()
             return carry
 
-        lax.fori_loop(0, ROWS, one, 0)
+        lax.fori_loop(0, GROUP, one, 0)
 
     attend(0)
     out.far(0)
     out.far(1)
-    for k in (2, 3):
-        out.from_plane(k, 0)
+    out.from_plane(2, 0)
+    out.from_plane(3, 0)
     attend(1)
-    for k in (2, 3):
-        out.from_plane(k, -1)
-        out.from_plane(k, 1)
-        out.from_plane(k, 2)
+    out.from_plane(2, -1)
+    out.from_plane(2, 1)
+    out.from_plane(3, -1)
+    out.from_plane(3, 1)
     attend(2)
+    out.from_plane(2, 2)
+    out.from_plane(3, 2)
+    attend(3)
     for k in range(4):
         out.await_sibling(k)
     await_bytes(gathered, att_recv)
@@ -396,9 +414,12 @@
         residual = jnp.dot(own_rows, embed3[third], preferred_element_type=F32)
         moved = residual + mod_row(2, 0, D) * updated[third * QROW : (third + 1) * QROW, :]
         normed.append(layer_norm(moved).astype(BF16))
-    near = jnp.dot(normed[0], final2[0], preferred_element_type=F32)
-    near = near + jnp.dot(normed[1], final2[1], preferred_element_type=F32)
-    rest = jnp.dot(normed[2], final2[0], preferred_element_type=F32)
+
+    def to_noise(rows, half):
+        return lax.dot_general(rows, final2[half], (((1,), (1,)), ((), ())), preferred_element_type=F32)
+
+    near = (to_noise(normed[0], 0) + to_noise(normed[1], 1)).astype(BF16)
+    rest = to_noise(normed[2], 0).astype(BF16)
     for k in range(8):
         at = slice(k * PACK, (k + 1) * PACK)
         noise_own[k, :, :HD] = near[at]
@@ -428,7 +449,7 @@
     sums = []
     for t in range(STEPS):
         previous = before if t == 0 else packed[t - 1]
-        running = running + (coef[t : t + 1, :] * previous + coef[STEPS + t : STEPS + t + 1, :] * noise_in[t])
+        running = running + (coef[t : t + 1, :] * previous + coef[STEPS + t : STEPS + t + 1, :] * noise_in[t].astype(F32))
         sums.append(running)
     total[...] = running
     for o in range(1, PLANES):
@@ -475,7 +496,9 @@
     pltpu.make_async_copy(part, parts.at[s], part_recv).start()
     await_bytes(parts, part_recv)
     summed = jnp.sum(jnp.sum(parts[...], axis=0), axis=1, keepdims=True) / (D * CH)
-    err_out[...] = jnp.broadcast_to(summed, (STEPS, HD))
+    row = lax.broadcasted_iota(jnp.int32, (STEPS, HD), 0)
+    lane = lax.broadcasted_iota(jnp.int32, (STEPS, HD), 1)
+    err_out[...] = jnp.sum(jnp.where(row == lane, summed, 0.0), axis=0, keepdims=True)
 
     qkv.finish()
     out.finish()
@@ -503,30 +526,30 @@
 def per_device(
     states, first_state, now_step, next_step, embed_weight, mod_weight, qkv_weight, out_weight, final_weight
 ):
-    plane = lax.axis_index("tm")
-    keep_coef, noise_coef = coefficients(now_step, next_step)
-    coef = jnp.broadcast_to(jnp.concatenate([keep_coef, noise_coef])[:, None], (2 * STEPS, LANES))
-    last = jnp.logical_and(plane == PLANES - 1, jnp.arange(STEPS) == STEPS - 1)
-    mods = modulation(jnp.where(last, 960, next_step), mod_weight)
-    qkv_pieces = jnp.transpose(qkv_weight.reshape(TOK, ROWS, GROUP * 3 * HD), (1, 0, 2))
-    out_pieces = out_weight[None]
+    vmem_in = pl.BlockSpec(memory_space=pltpu.VMEM)
+    smem_in = pl.BlockSpec(memory_space=pltpu.SMEM)
+    hbm_in = pl.BlockSpec(memory_space=pltpu.HBM)
     dma = pltpu.SemaphoreType.DMA
     vmem = pltpu.VMEM
     advanced, errors = pl.pallas_call(
         kernel,
         out_shape=(
             jax.ShapeDtypeStruct((STEPS, TOK, CH), F32),
-            jax.ShapeDtypeStruct((STEPS, HD), F32),
+            jax.ShapeDtypeStruct((1, HD), F32),
         ),
-        in_specs=[pl.BlockSpec(memory_space=pltpu.VMEM)] * 8,
+        in_specs=[vmem_in, vmem_in, smem_in, smem_in, vmem_in, hbm_in, vmem_in, vmem_in, vmem_in],
         out_specs=(pl.BlockSpec(memory_space=pltpu.VMEM),) * 2,
         scratch_shapes=[
+            vmem((256, 3 * D), BF16),
+            vmem((STEPS, 3 * D), F32),
+            vmem((2 * STEPS, LANES), F32),
+            vmem((ROWS, TOK, GROUP * 3 * HD), BF16),
             vmem((STEPS, PACK, LANES), F32),
             vmem((STEPS, PACK, LANES), BF16),
             vmem((PEERS * PACK, LANES), BF16),
             vmem((PACK, LANES), F32),
             vmem((3, LANES, D), BF16),
-            vmem((2, D, HD), BF16),
+            vmem((2, HD, D), BF16),
             vmem((D, GROUP * 3 * HD), BF16),
             vmem((D, D), BF16),
             vmem((D, D), BF16),
@@ -537,8 +560,8 @@
             vmem((GROUP * ROWS, QTOK, HD), BF16),
             vmem((QTOK, D), BF16),
             vmem((QTOK, D), F32),
-            vmem((8, PACK, LANES), F32),
-            vmem((STEPS, PACK, LANES), F32),
+            vmem((8, PACK, LANES), BF16),
+            vmem((STEPS, PACK, LANES), BF16),
             vmem((PACK, LANES), F32),
             vmem((PLANES, PACK, LANES), F32),
             vmem((STEPS, HD), F32),
@@ -546,14 +569,17 @@
             dma((PEERS,)), dma, dma,
             dma((PEERS,)), dma, dma,
             dma, dma, dma, dma, dma, dma,
-            dma, dma, dma((PLANES,)), dma((PLANES,)), dma, dma,
+            dma, dma, dma, dma((PLANES,)), dma((PLANES,)), dma, dma,
         ],
         compiler_params=pltpu.CompilerParams(
             collective_id=0, has_side_effects=True, vmem_limit_bytes=60 * 1024 * 1024
         ),
         name="picard",
-    )(states, first_state, mods, coef, embed_weight, qkv_pieces, out_pieces, final_weight)
-    return advanced, errors[:, 0]
+    )(
+        states, first_state, now_step, next_step, embed_weight, mod_weight,
+        jnp.transpose(qkv_weight, (1, 0, 2)), out_weight[None], final_weight.T,
+    )
+    return advanced, errors[0, :STEPS]
 
 
 def solution(mesh):

time: 92.4 us -> 83.5 us (0.904)
  local copies, waits for them, and re-layouts: 7.43 us -> 2.75 us
  Pallas kernels: 80.9 us -> 78.5 us
  other arithmetic: 1.14 us -> 0 us
  matrix products: 1.08 us -> 0 us
    unnamed x11 -> x1, local copies, waits for them, and re-layouts: 4.29 us -> 1.62 us
    pallas_call x1, Pallas kernels: 80.9 us -> 78.5 us  [per_device(): pl.pallas_call(kernel, out_shape=(jax.ShapeDtypeStruct((STEPS, TOK, CH),...]
    slice x1 -> x0, local copies, waits for them, and re-layouts: 1.31 us -> none  [per_device(): return (advanced, errors[:, 0])]
    reshape x2 -> x0, local copies, waits for them, and re-layouts: 1.14 us -> none  [per_device(): qkv_weight.reshape(TOK, ROWS, GROUP * 3 * HD)]
    squeeze x0 -> x1, local copies, waits for them, and re-layouts: none -> 1.13 us  [per_device(): return (advanced, errors[0, :STEPS])]
    dot_general x1 -> x0, matrix products: 1.08 us -> none  [modulation(): return jnp.dot(time_embed, mod_weight, preferred_element_type=F32)]
where the time goes in v2:
time: 83.5 us; the launch traced here: 81.9 us
  Pallas kernels  78.5 us (94%)
  local copies, waits for them, and re-layouts  2.75 us (3%)
    pallas_call x1, Pallas kernels, per_device(): pl.pallas_call(kernel, out_shape=(jax.ShapeDtypeStruct((STEPS, TOK, CH),...  78.5 us

profile of v2, /device:TPU:1, one launch (start us, length us, event | category | flops | bytes accessed | tf_op | source)
XLA Modules:
  0.0 81.9 jit_solution(1438152160839588471)
XLA Ops:
  0.6 78.5 %picard.1 = (f32[8,48,64]{2,1,0:T(8,128)}, f32[1,128]{1,0:T(1,128)}) custom-call(f32[8,48,64]{2,1,0:T(8,128)} %states.1, f32[48,64]{1,0:T(8,128)} %first.1, s32[8]{0:T(128)} %now_step.1, s32[8]{0:T(128)} %next_step.1, bf16[64,1536]{1,0:T(8,128)(2,1)} %embed.1, bf16[256,4608]{1,0:T(8,128)(2,1)} %mod_weight.1, bf16[12,48,384]{2,1,0:T(8,128)(2,1)} %bitcast.5, ...), custom_call_target="tpu_custom_call" | custom-call | tf_op jit(solution)/shard_map/picard/pallas_call | solution.py:534
  79.2 1.1 %slice_bitcast_fusion = f32[8]{0:T(128)} fusion(f32[1,128]{1,0:T(1,128)} %get-tuple-element.5), kind=kLoop, calls=%fused_computation | loop fusion | bytes 64 | tf_op jit(solution)/shard_map/squeeze | solution.py:582
  80.3 1.6 %copy.12 = f32[8,48,64]{2,1,0:T(8,128)} copy(f32[8,48,64]{2,1,0:T(8,128)} %get-tuple-element.8) | data formatting | bytes 196608
